TPU v7x, 32 devices: a whole 2x2x4 slice. The times are simulated.
32 devices in a mesh: corpus: 4 (over z), rerank: 8 (over y, x, core).
Axes of the slice: x: 2, y: 2, z: 4, core: 2. Of those that a mesh axis runs over, the one named last changes fastest.
Arguments:
- store_rows: bfloat16 [128, 512, 3584], P('corpus', 'rerank'), may hold values from -400 to 400
- block_lengths: int32 [128], replicated, may hold values from 128 to 512
- queries: bfloat16 [32, 64, 3584], P(None, 'rerank'), may hold values from -400 to 400
- cand_owner: int32 [64, 1], replicated, may hold values from 0 to 3; in each aligned block of 16 rows (0 to 15, 16 to 31, ...) at most 5 rows name the same one
- cand_block: int32 [64], replicated, may hold values from 0 to 31
- cand_query: int32 [64], replicated, may hold values from 0 to 31
- norm_gain: bfloat16 [3584], replicated, may hold values from 0.099609375 to 1.8984375
- w_query: bfloat16 [3584, 1792], P('rerank'), may hold values from -8 to 8
- w_key: bfloat16 [3584, 256], P('rerank'), may hold values from -1 to 1
- w_value: bfloat16 [3584, 256], P('rerank'), may hold values from -0.09375 to 0.09375
- w_score: bfloat16 [1792], replicated, may hold values from -0.125 to 0.125
Outputs:
- passage_context: bfloat16 [80, 512, 1792], P('corpus', 'rerank')
- pair_scores: float32 [64], P(('corpus', 'rerank'))
Inputs may be any that keep to these rules, and one draw needn't show every extreme that they name: `cand_owner`: at most 5 of the 16 pairs of one corpus group (an aligned block of rows) name the same owner, in every draw, some group names one owner in exactly 5 of its 16 pairs.
All inputs are finite; a program needn't handle non-finite values.
Results may differ from a plain program's by a relative error of at most 0.013.
Values may be sent and summed in bfloat16 or wider, within the bound.
A program may use at most 128 MiB of HBM per device.

v0:
```python
import jax
import jax.numpy as jnp
from jax import lax
from jax.sharding import PartitionSpec as P

HDIM = 128
QHEADS = 14
KVHEADS = 2
BLK = 512
CAP = 5
ROPE_BASE = 1000000.0
EPSILON = 1e-06


def rotate(values, positions):
    head_dim = values.shape[-1]
    half_dim = head_dim // 2
    inverse = jnp.power(ROPE_BASE, -2.0 * jnp.arange(half_dim, dtype=jnp.float32) / head_dim)
    angles = positions.astype(jnp.float32)[..., None] * inverse
    cosine = jnp.cos(angles)[..., None, :]
    sine_part = jnp.sin(angles)[..., None, :]
    lower = values[..., :half_dim]
    upper = values[..., half_dim:]
    return jnp.concatenate(
        [lower * cosine - upper * sine_part, upper * cosine + lower * sine_part], axis=-1
    )


def pick_rows(table, wanted, indices):
    present = jnp.any(wanted, axis=1)
    picked = jnp.sum(jnp.where(wanted, indices[None, :], 0), axis=1)
    chosen = jnp.take(table, picked, axis=0)
    return jnp.where(present[:, None, None], chosen, jnp.zeros((), table.dtype))


def add_products(pieces, columns):
    return (
        jnp.dot(columns, pieces[0], preferred_element_type=jnp.float32),
        jnp.dot(columns, pieces[1], preferred_element_type=jnp.float32),
        jnp.dot(columns, pieces[2], preferred_element_type=jnp.float32),
    )


def attend_one(items):
    query_rot, key_rot, values, length = items
    seq_len = query_rot.shape[0]
    token_ids = jnp.arange(seq_len, dtype=jnp.int32)
    grouped = query_rot.reshape(seq_len, KVHEADS, QHEADS // KVHEADS, HDIM)
    logits = jnp.einsum(
        "skgd,tkd->kgst", grouped, key_rot, preferred_element_type=jnp.float32
    ) * HDIM ** (-0.5)
    live = (token_ids < length) | (token_ids >= BLK)
    allowed = live[None, :] & (token_ids[None, :] <= token_ids[:, None])
    masked = jnp.where(allowed, logits, -1e30)
    peak = jnp.max(masked, axis=-1, keepdims=True)
    weights = jnp.where(allowed, jnp.exp(masked - peak), 0.0)
    probs = (weights / jnp.sum(weights, axis=-1, keepdims=True)).astype(jnp.bfloat16)
    context = jnp.einsum("kgst,tkd->skgd", probs, values, preferred_element_type=jnp.float32)
    return context.reshape(seq_len, QHEADS * HDIM).astype(jnp.bfloat16)


def on_device(
    store_rows,
    block_lengths,
    queries,
    cand_owner,
    cand_block,
    cand_query,
    norm_gain,
    w_query,
    w_key,
    w_value,
    w_score,
):
    n_corpus = lax.axis_size("corpus")
    n_rerank = lax.axis_size("rerank")
    corpus_index = lax.axis_index("corpus")
    member = lax.axis_index("rerank")
    pair_total = cand_block.shape[0]
    pair_group = pair_total // n_corpus
    pair_dev = pair_group // n_rerank
    own_blocks = store_rows.shape[0]
    owners = cand_owner[:, 0]
    pair_order = jnp.arange(pair_total, dtype=jnp.int32)
    group_of = pair_order // pair_group
    earlier = (
        (owners[:, None] == owners[None, :])
        & (group_of[:, None] == group_of[None, :])
        & (pair_order[None, :] < pair_order[:, None])
    )
    owner_rank = jnp.sum(earlier.astype(jnp.int32), axis=1)
    slot_ids = jnp.arange(n_corpus * CAP, dtype=jnp.int32)
    slot_group = slot_ids // CAP
    slot_rank = slot_ids % CAP
    wanted = (
        (group_of[None, :] == slot_group[:, None])
        & (owners[None, :] == corpus_index)
        & (owner_rank[None, :] == slot_rank[:, None])
    )
    outgoing = pick_rows(store_rows, wanted, cand_block)
    arrived = lax.all_to_all(outgoing, "corpus", split_axis=0, concat_axis=0, tiled=True)
    local_pairs = corpus_index * pair_group + jnp.arange(pair_group, dtype=jnp.int32)
    local_owner = jnp.take(owners, local_pairs)
    local_rank = jnp.take(owner_rank, local_pairs)
    passages = jnp.take(arrived, local_owner * CAP + local_rank, axis=0)
    query_rows = jnp.take(queries, jnp.take(cand_query, local_pairs), axis=0)
    passage_rows, question_rows = (
        lax.all_to_all(passages, "rerank", split_axis=0, concat_axis=1, tiled=True),
        lax.all_to_all(query_rows, "rerank", split_axis=0, concat_axis=1, tiled=True),
    )
    joined = jnp.concatenate([passage_rows, question_rows], axis=1)
    device_pairs = (
        corpus_index * pair_group + member * pair_dev + jnp.arange(pair_dev, dtype=jnp.int32)
    )
    lengths = jnp.take(
        block_lengths,
        jnp.take(owners, device_pairs) * own_blocks + jnp.take(cand_block, device_pairs),
    )
    seq_len = joined.shape[1]
    width = joined.shape[2]
    row_count = pair_dev * seq_len
    widened = joined.astype(jnp.float32)
    inverse_rms = lax.rsqrt(jnp.mean(widened * widened, axis=-1, keepdims=True) + EPSILON)
    normed = (
        (widened * inverse_rms * norm_gain.astype(jnp.float32))
        .astype(jnp.bfloat16)
        .reshape(row_count, width)
    )
    query_raw, key_raw, value_raw = add_products(
        (
            lax.all_gather(w_query, "rerank", axis=0, tiled=True),
            lax.all_gather(w_key, "rerank", axis=0, tiled=True),
            lax.all_gather(w_value, "rerank", axis=0, tiled=True),
        ),
        normed,
    )
    token_ids = jnp.arange(seq_len, dtype=jnp.int32)
    positions = jnp.where(
        token_ids[None, :] < BLK, token_ids[None, :], lengths[:, None] + token_ids[None, :] - BLK
    )
    query_rot = rotate(query_raw.reshape(pair_dev, seq_len, QHEADS, HDIM), positions).astype(
        jnp.bfloat16
    )
    key_rot = rotate(key_raw.reshape(pair_dev, seq_len, KVHEADS, HDIM), positions).astype(
        jnp.bfloat16
    )
    values = value_raw.reshape(pair_dev, seq_len, KVHEADS, HDIM).astype(jnp.bfloat16)
    context = lax.map(attend_one, (query_rot, key_rot, values, lengths))
    pair_scores = jnp.dot(context[:, seq_len - 1, :], w_score, preferred_element_type=jnp.float32)
    keep = token_ids[None, :BLK] < lengths[:, None]
    passage_context = jnp.where(keep[:, :, None], context[:, :BLK], jnp.zeros((), jnp.bfloat16))
    returned = lax.all_to_all(passage_context, "rerank", split_axis=1, concat_axis=0, tiled=True)
    home_want = (local_owner[None, :] == slot_group[:, None]) & (
        local_rank[None, :] == slot_rank[:, None]
    )
    homebound = pick_rows(returned, home_want, jnp.arange(pair_group, dtype=jnp.int32))
    landed = lax.all_to_all(homebound, "corpus", split_axis=0, concat_axis=0, tiled=True)
    return (landed, pair_scores)


def solution(mesh):
    placed = (
        P("corpus", "rerank", None),
        P(),
        P(None, "rerank", None),
        P(),
        P(),
        P(),
        P(),
        P("rerank", None),
        P("rerank", None),
        P("rerank", None),
        P(),
    )
    return jax.shard_map(
        on_device,
        mesh=mesh,
        in_specs=placed,
        out_specs=(P("corpus", "rerank", None), P(("corpus", "rerank"))),
        check_vma=False,
    )
```

profile of v0, /device:TPU:2, one launch (start us, length us, event | category | flops | bytes accessed | tf_op | source)
XLA Modules:
  0.0 673.4 jit_solution(5403517321702879606)
XLA Ops:
  7.2 0.7 all-gather.6.cloned.1.call-update
  8.0 0.7 all-gather.4.cloned.1.call-update
  8.7 0.7 broadcast_compare_fusion.1
  9.4 0.9 convert_reduce_fusion
  10.3 0.8 select_reduce_fusion
  11.4 11.1 %gather_fusion.1 = bf16[20,64,3584]{2,1,0:T(8,128)(2,1)} fusion(bf16[32,64,3584]{2,1,0:T(8,128)(2,1)} %param.17, s32[1024]{0:T(1024)S(1)} %pad_clamp_fusion.3), kind=kCustom, calls=%fused_computation.6 | custom fusion | bytes 18350160 | tf_op jit(solution)/shard_map/jit(_take)/gather | solution.py:32
  22.5 8.2 %select_select_fusion = bf16[20,64,3584]{2,1,0:T(8,128)(2,1)} fusion(bf16[20,64,3584]{2,1,0:T(8,128)(2,1)} %gather_fusion.1, pred[20]{0:T(512)(128)(4,1)S(1)} %compare_and_fusion.5, pred[20]{0:T(512)(128)(4,1)S(1)} %fusion.35), kind=kLoop, calls=%fused_computation.45 | loop fusion | flops 9175040 | bytes 18350120 | tf_op jit(solution)/shard_map/jit(_where)/select_n | solution.py:33
  30.7 5.9 all-to-all-start
  36.6 0.7 all-gather.8.cloned.1.call-update
  37.4 0.7 gather_fusion.6
  38.0 0.7 gather_fusion.5
  38.7 0.7 gather_fusion.9
  40.6 1.1 broadcast_select_fusion.2
  41.7 195.2 %all-to-all-done = bf16[20,64,3584]{2,1,0:T(8,128)(2,1)} async-done(((bf16[20,64,3584]{2,1,0:T(8,128)(2,1)}), bf16[20,64,3584]{2,1,0:T(8,128)(2,1)}, u32[]{:S(2)}, u32[]{:S(2)}) %all-to-all-start) | async-done | bytes 9175072 | tf_op jit(solution)/shard_map/all_to_all | solution.py:101
  236.8 4.2 all-to-all-start.2
  241.1 7.6 %gather_fusion.2 = bf16[16,64,3584]{2,1,0:T(8,128)(2,1)} fusion(bf16[20,64,3584]{2,1,0:T(8,128)(2,1)} %all-to-all-done, s32[1024]{0:T(1024)S(1)} %pad_clamp_fusion.2), kind=kCustom, calls=%fused_computation.7 | custom fusion | bytes 14680128 | tf_op jit(solution)/shard_map/jit(_take)/gather | solution.py:105
  248.7 6.9 %broadcast_select_fusion = bf16[16,64,3584]{2,1,0:T(8,128)(2,1)} fusion(bf16[16,64,3584]{2,1,0:T(8,128)(2,1)} %gather_fusion.2, pred[16]{0:T(512)(128)(4,1)S(1)} %get-tuple-element.63), kind=kLoop, calls=%fused_computation.50 | loop fusion | flops 3670016 | bytes 14680080 | tf_op jit(solution)/shard_map/jit(_take)/select_n | solution.py:105
  255.6 5.2 all-to-all-start.1
  260.9 0.6 gather_fusion.7
  261.5 0.6 gather_fusion.8
  262.2 0.6 gather_fusion
  263.0 0.8 broadcast_compare_fusion
  263.7 2.1 multiply_cosine_fusion
  265.8 1.0 copy.62
  266.8 3.8 copy.49
  270.6 3.8 copy.48
  274.4 67.8 %all-to-all-done.1 = bf16[16,64,3584]{2,1,0:T(8,128)(2,1)} async-done(((bf16[16,64,3584]{2,1,0:T(8,128)(2,1)}), bf16[16,64,3584]{2,1,0:T(8,128)(2,1)}, u32[]{:S(2)}, u32[]{:S(2)}) %all-to-all-start.1) | async-done | bytes 7340064 | tf_op jit(solution)/shard_map/all_to_all | solution.py:108
  342.2 3.8 copy.46
  346.0 2.0 fusion.30
  348.0 0.8 copy-done.9
  348.9 2.4 fusion.41
  352.1 3.4 convolution_convert_fusion
  355.5 18.0 %copy.50 = bf16[1792,3584]{1,0:T(8,128)(2,1)} copy(bf16[1792,3584]{0,1:T(8,128)(2,1)} %bitcast.115) | data formatting | bytes 25690112 | tf_op jit(solution)/shard_map/dot_general | solution.py:38
  373.5 23.9 %fusion.39 = f32[2,576,14,128]{3,1,2,0:T(8,128)} fusion(bf16[14,128,3584,1]{2,1,0,3:T(8,128)(2,1)} %bitcast.116, f32[3584]{0:T(1024)S(1)} %convert_element_type.66, f32[2,576]{1,0:T(2,128)S(1)} %add_rsqrt_fusion, bf16[2,64,3584]{2,1,0:T(8,128)(2,1)S(1)} %bitcast.121, bf16[2,512,3584]{2,1,0:T(8,128)(2,1)} %bitcast.112), kind=kOutput, calls=%fused_computation.117 | convolution fusion | flops 14826405888 | bytes 29379072 | tf_op jit(solution)/shard_map/dot_general | solution.py:38
  397.4 8.6 %subtract_convert_fusion = (bf16[2,576,14,64]{3,1,2,0:T(8,128)(2,1)S(1)}, bf16[2,576,14,64]{3,1,2,0:T(8,128)(2,1)S(1)}) fusion(f32[2,576,14,128]{3,1,2,0:T(8,128)} %fusion.39, f32[2,576,64]{2,1,0:T(8,128)S(1)} %get-tuple-element.62, f32[2,576,64]{2,1,0:T(8,128)S(1)} %get-tuple-element.61), kind=kLoop, calls=%fused_computation.49 | loop fusion | flops 8257536 | bytes 12976128 | tf_op jit(solution)/shard_map/convert.2
  405.9 4.3 pad_maximum_fusion.1
  410.2 69.3 %while.10 = (s32[]{:T(128)}, bf16[2,576,1792]{2,1,0:T(8,128)(2,1)}, bf16[2,576,2,128]{3,1,2,0:T(8,128)(2,1)}, s32[2]{0:T(128)S(1)}, bf16[2,576,2,128]{3,1,2,0:T(...) while((s32[]{:T(128)}, bf16[2,576,1792]{2,1,0:T(8,128)(2,1)}, ...), condition=%wide.region_9.12_spmd, body=%wide.region_6.11_spmd.sunk | while | flops 2412382464 | bytes 61592804 | solution.py:148
  410.4 1.7 constant_dynamic-slice_fusion.2
  412.7 0.6 fusion.64
  413.5 12.5 %fusion.66 = (f32[2,7,576]{2,1,0:T(8,128)S(1)}, f32[2,7,576,576]{2,3,1,0:T(8,128)}) fusion(pred[576,576]{0,1:T(8,128)(4,1)S(1)} %fusion.65, bf16[576,2,7,128]{3,0,2,1:T(8,128)(2,1)S(1)} %bitcast.108, bf16[2,576,2,128]{3,1,2,0:T(8,128)(2,1)S(1)} %get-tuple-element.128, s32[]{:T(128)} %get-tuple-element.117), kind=kOutput, calls=%fused_computation.119.clone.1 | convolution fusion | flops 1212310016 | bytes 21708292 | tf_op jit(solution)/shard_map/while/body/eval_jaxpr/sub | solution.py:56
  426.0 11.1 %convert_bitcast_fusion.2 = bf16[576,2,7,128]{3,0,2,1:T(8,128)(2,1)S(1)} fusion(f32[2,7,576,576]{2,3,1,0:T(8,128)} %get-tuple-element.108, f32[2,7,576]{2,1,0:T(8,128)S(1)} %get-tuple-element.109, bf16[2,576,2,128]{3,1,2,0:T(8,128)(2,1)} %get-tuple-element.126, s32[]{:T(128)} %get-tuple-element.117), kind=kOutput, calls=%fused_computation.19.clone.1 | convolution fusion | flops 1199407104 | bytes 23035904 | tf_op jit(solution)/shard_map/while/body/eval_jaxpr/kgst,tkd->skgd/dot_general | solution.py:58
  437.1 1.4 copy.64
  438.5 3.3 convert_element_type.102
  441.8 3.0 constant_dynamic-update-slice_fusion.2
  444.8 1.7 constant_dynamic-slice_fusion.2
  447.2 0.6 fusion.64
  448.0 12.5 %fusion.66 = (f32[2,7,576]{2,1,0:T(8,128)S(1)}, f32[2,7,576,576]{2,3,1,0:T(8,128)}) fusion(pred[576,576]{0,1:T(8,128)(4,1)S(1)} %fusion.65, bf16[576,2,7,128]{3,0,2,1:T(8,128)(2,1)S(1)} %bitcast.108, bf16[2,576,2,128]{3,1,2,0:T(8,128)(2,1)S(1)} %get-tuple-element.128, s32[]{:T(128)} %get-tuple-element.117), kind=kOutput, calls=%fused_computation.119.clone.1 | convolution fusion | flops 1212310016 | bytes 21708292 | tf_op jit(solution)/shard_map/while/body/eval_jaxpr/sub | solution.py:56
  460.5 11.1 %convert_bitcast_fusion.2 = bf16[576,2,7,128]{3,0,2,1:T(8,128)(2,1)S(1)} fusion(f32[2,7,576,576]{2,3,1,0:T(8,128)} %get-tuple-element.108, f32[2,7,576]{2,1,0:T(8,128)S(1)} %get-tuple-element.109, bf16[2,576,2,128]{3,1,2,0:T(8,128)(2,1)} %get-tuple-element.126, s32[]{:T(128)} %get-tuple-element.117), kind=kOutput, calls=%fused_computation.19.clone.1 | convolution fusion | flops 1199407104 | bytes 23035904 | tf_op jit(solution)/shard_map/while/body/eval_jaxpr/kgst,tkd->skgd/dot_general | solution.py:58
  471.6 1.4 copy.64
  473.0 3.3 convert_element_type.102
  476.3 3.0 constant_dynamic-update-slice_fusion.2
  479.5 6.4 copy.51
  486.0 5.7 broadcast_select_fusion.1
  491.7 5.9 all-to-all-start.3
  497.8 41.8 %all-to-all-done.3 = bf16[2,512,1792]{2,0,1:T(2,128)(2,1)} async-done(((bf16[2,512,1792]{2,0,1:T(2,128)(2,1)}), bf16[2,512,1792]{2,0,1:T(2,128)(2,1)}, u32[]{:S(2)}, u32[]{:S(2)}) %all-to-all-start.3) | async-done | bytes 3670048 | tf_op jit(solution)/shard_map/all_to_all | solution.py:152
  539.7 2.5 copy.52
  542.2 2.1 copy.53
  544.3 5.3 gather_fusion.4
  549.5 5.1 select_select_fusion.1
  554.7 4.9 all-to-all-start.4
  559.7 0.8 slice.27
  560.5 0.6 convolution_bitcast_fusion
  561.1 100.6 %all-to-all-done.4 = bf16[20,64,1792]{2,1,0:T(8,128)(2,1)} async-done(((bf16[20,64,1792]{2,1,0:T(8,128)(2,1)}), bf16[20,64,1792]{2,1,0:T(8,128)(2,1)}, u32[]{:S(2)}, u32[]{:S(2)}) %all-to-all-start.4) | async-done | bytes 4587552 | tf_op jit(solution)/shard_map/all_to_all | solution.py:157
  661.8 4.9 copy.75
  (81 shorter events, 4.4 us)
Async XLA Ops:
  7.2 32.8 %copy-start = (bf16[32,8,3584]{2,1,0:T(8,128)(2,1)S(1)}, bf16[32,8,3584]{2,1,0:T(8,128)(2,1)}, u32[]{:S(2)}) copy-start(bf16[32,8,3584]{2,1,0:T(8,128)(2,1)} %param.19) | copy-start | bytes 5505028
  7.2 259.6 %all-gather.6.cloned.1.call-start = ((), (), s32[]{:S(2)}) async-start(), calls=%async_computation.6 | async-start | bytes 2064384 | tf_op jit(solution)/shard_map/all_gather | solution.py:132
  7.9 262.7 %all-gather.4.cloned.1.call-start = ((), (), s32[]{:S(2)}) async-start(), calls=%async_computation.5 | async-start | bytes 2064384 | tf_op jit(solution)/shard_map/all_gather | solution.py:133
  8.7 13.8 %copy-start.12 = (s32[20]{0:T(128)}, s32[20]{0:T(128)S(1)}, u32[]{:S(2)}) copy-start(s32[20]{0:T(128)S(1)} %get-tuple-element.67) | copy-start | bytes 244
  8.7 13.8 %copy-start.14 = (s32[20]{0:T(128)}, s32[20]{0:T(128)S(1)}, u32[]{:S(2)}) copy-start(s32[20]{0:T(128)S(1)} %get-tuple-element.68) | copy-start | bytes 244
  30.7 7.3 %copy-start.2 = (s32[64,1]{0,1:T(1,128)S(1)}, s32[64,1]{0,1:T(1,128)}, u32[]{:S(2)}) copy-start(s32[64,1]{0,1:T(1,128)} %param.20) | copy-start | bytes 772
  30.7 8.0 %copy-start.4 = (s32[64]{0:T(128)S(1)}, s32[64]{0:T(128)}, u32[]{:S(2)}) copy-start(s32[64]{0:T(128)} %param.22) | copy-start | bytes 772
  30.7 206.1 %all-to-all-start = ((bf16[20,64,3584]{2,1,0:T(8,128)(2,1)}), bf16[20,64,3584]{2,1,0:T(8,128)(2,1)}, u32[]{:S(2)}, u32[]{:S(2)}) async-start(bf16[20,64,3584]{2,1,0:T(8,128)(2,1)} %select_select_fusion), calls=%async_computation | async-start | bytes 18350080 | tf_op jit(solution)/shard_map/all_to_all | solution.py:101
  36.6 318.9 %all-gather.8.cloned.1.call-start = ((), (), s32[]{:S(2)}) async-start(), calls=%async_computation.7 | async-start | bytes 14450688 | tf_op jit(solution)/shard_map/all_gather | solution.py:131
  236.8 18.7 %all-to-all-start.2 = ((bf16[16,8,3584]{2,1,0:T(8,128)(2,1)}), bf16[16,8,3584]{2,1,0:T(8,128)(2,1)S(1)}, u32[]{:S(2)}, u32[]{:S(2)}) async-start(bf16[16,8,3584]{2,1,0:T(8,128)(2,1)} %broadcast_select_fusion.2), calls=%async_computation.2 | async-start | bytes 1835008 | tf_op jit(solution)/shard_map/all_to_all | solution.py:109
  255.6 5.9 copy-start.3
  255.6 6.6 copy-start.11
  255.6 6.6 copy-start.5
  255.6 86.6 %all-to-all-start.1 = ((bf16[16,64,3584]{2,1,0:T(8,128)(2,1)}), bf16[16,64,3584]{2,1,0:T(8,128)(2,1)}, u32[]{:S(2)}, u32[]{:S(2)}) async-start(bf16[16,64,3584]{2,1,0:T(8,128)(2,1)} %broadcast_select_fusion), calls=%async_computation.1 | async-start | bytes 14680064 | tf_op jit(solution)/shard_map/all_to_all | solution.py:108
  342.2 3.8 copy-start.7
  346.0 6.1 copy-start.6
  346.0 2.9 copy-start.9
  348.9 3.2 copy-start.8
  479.5 6.5 copy-start.10
  486.0 11.6 %copy-start.13 = (s32[20]{0:T(128)S(1)}, s32[20]{0:T(128)}, u32[]{:S(2)}) copy-start(s32[20]{0:T(128)} %copy-done.12) | copy-start | bytes 244
  486.0 11.6 %copy-start.15 = (s32[20]{0:T(128)S(1)}, s32[20]{0:T(128)}, u32[]{:S(2)}) copy-start(s32[20]{0:T(128)} %copy-done.14) | copy-start | bytes 244
  486.0 11.6 %copy-start.16 = (s32[16]{0:T(128)S(1)}, s32[16]{0:T(128)}, u32[]{:S(2)}) copy-start(s32[16]{0:T(128)} %get-tuple-element.65) | copy-start | bytes 196
  486.0 11.6 %copy-start.17 = (s32[16]{0:T(128)S(1)}, s32[16]{0:T(128)}, u32[]{:S(2)}) copy-start(s32[16]{0:T(128)} %get-tuple-element.66) | copy-start | bytes 196
  491.7 48.0 %all-to-all-start.3 = ((bf16[2,512,1792]{2,0,1:T(2,128)(2,1)}), bf16[2,512,1792]{2,0,1:T(2,128)(2,1)}, u32[]{:S(2)}, u32[]{:S(2)}) async-start(bf16[2,512,1792]{2,0,1:T(2,128)(2,1)} %broadcast_select_fusion.1), calls=%async_computation.3 | async-start | bytes 7340032 | tf_op jit(solution)/shard_map/all_to_all | solution.py:152
  549.5 10.1 %copy-start.18 = (bf16[1792]{0:T(1024)(128)(2,1)S(1)}, bf16[1792]{0:T(1024)(128)(2,1)}, u32[]{:S(2)}) copy-start(bf16[1792]{0:T(1024)(128)(2,1)} %param.27) | copy-start | bytes 10756
  549.5 117.1 %copy-start.1 = (bf16[32,8,3584]{2,1,0:T(8,128)(2,1)S(1)}, bf16[32,8,3584]{2,1,0:T(8,128)(2,1)}, u32[]{:S(2)}) copy-start(bf16[32,8,3584]{2,1,0:T(8,128)(2,1)} %param.19) | copy-start | bytes 5505028
  554.7 107.1 %all-to-all-start.4 = ((bf16[20,64,1792]{2,1,0:T(8,128)(2,1)}), bf16[20,64,1792]{2,1,0:T(8,128)(2,1)}, u32[]{:S(2)}, u32[]{:S(2)}) async-start(bf16[20,64,1792]{2,1,0:T(8,128)(2,1)} %select_select_fusion.1), calls=%async_computation.4 | async-start | bytes 9175040 | tf_op jit(solution)/shard_map/all_to_all | solution.py:157
Sparse Core Ops, SparseCore 0:
  9.9 27.8 all-gather.5
  39.7 26.6 all-gather.3
  68.3 73.0 all-gather.7
where the time goes:
time: 679 us; the launch traced here: 673 us
  waiting for transfers between devices  407 us (60%)
  local copies, waits for them, and re-layouts  96.6 us (14%)
  matrix products  77.5 us (11%)
  other arithmetic  50.7 us (7%)
  starting transfers between devices  26.3 us (4%)
  between operations  14.4 us (2%)
    all_to_all x1, waiting for transfers between devices, on_device(): lax.all_to_all(outgoing, 'corpus', split_axis=0, concat_axis=0, tiled=True)  195 us
    all_to_all x1, waiting for transfers between devices, on_device(): lax.all_to_all(homebound, 'corpus', split_axis=0, concat_axis=0, tiled=True)  101 us
    all_to_all x1, waiting for transfers between devices, on_device(): lax.all_to_all(passages, 'rerank', split_axis=0, concat_axis=1, tiled=True)  67.8 us
    all_to_all x1, waiting for transfers between devices, on_device(): lax.all_to_all(passage_context, 'rerank', split_axis=1, concat_axis=0, ti...  41.8 us
    sub x2, matrix products, attend_one(): weights = jnp.where(allowed, jnp.exp(masked - peak), 0.0)  25 us
    dot_general x1, matrix products, add_products(): jnp.dot(columns, pieces[0], preferred_element_type=jnp.float32)  23.9 us
    dot_general x2, matrix products, attend_one(): jnp.einsum('kgst,tkd->skgd', probs, values, preferred_element_type=jnp.fl...  22.2 us
    dot_general x1, local copies, waits for them, and re-layouts, add_products(): jnp.dot(columns, pieces[0], preferred_element_type=jnp.float32)  18 us
  transfers between devices with their start and end apart: 8, of which 4 were waited for; matrix products, arithmetic and copies ran while one was open for 10% of the time, Pallas kernels for 0%

commit v1 on v0

--- a/solution.py
+++ b/solution.py
@@ -105,7 +105,12 @@
     passages = jnp.take(arrived, local_owner * CAP + local_rank, axis=0)
     query_rows = jnp.take(queries, jnp.take(cand_query, local_pairs), axis=0)
     passage_rows, question_rows = (
-        lax.all_to_all(passages, "rerank", split_axis=0, concat_axis=1, tiled=True),
+        jnp.concatenate(
+            lax.all_to_all(
+                jnp.stack(jnp.split(passages, lax.axis_size("rerank"), axis=0)), "rerank", 0, 0
+            ),
+            axis=1,
+        ),
         lax.all_to_all(query_rows, "rerank", split_axis=0, concat_axis=1, tiled=True),
     )
     joined = jnp.concatenate([passage_rows, question_rows], axis=1)

time: 679 us -> 696 us (1.025)
  local copies, waits for them, and re-layouts: 96.6 us -> 105 us
  other arithmetic: 50.7 us -> 58.9 us
    another operation x2, other arithmetic: 9.03 us -> 19.2 us
    unnamed x40 -> x45, local copies, waits for them, and re-layouts: 5.8 us -> 12.9 us
  transfers between devices with their start and end apart: 8 -> 8, of which waited for: 4 -> 4; matrix products, arithmetic and copies ran while one was open for 10% -> 7% of each run, Pallas kernels for 0% -> 0%
where the time goes in v1:
time: 696 us; the launch traced here: 690 us
  waiting for transfers between devices  408 us (59%)
  local copies, waits for them, and re-layouts  105 us (15%)
  matrix products  77 us (11%)
  other arithmetic  58.9 us (8%)
  starting transfers between devices  26.4 us (4%)
  between operations  14.4 us (2%)
    all_to_all x1, waiting for transfers between devices, on_device(): lax.all_to_all(outgoing, 'corpus', split_axis=0, concat_axis=0, tiled=True)  194 us
    all_to_all x1, waiting for transfers between devices, on_device(): lax.all_to_all(homebound, 'corpus', split_axis=0, concat_axis=0, tiled=True)  101 us
    all_to_all x1, waiting for transfers between devices, on_device(): lax.all_to_all(jnp.stack(jnp.split(passages, lax.axis_size('rerank'), axi...  69.9 us
    all_to_all x1, waiting for transfers between devices, on_device(): lax.all_to_all(passage_context, 'rerank', split_axis=1, concat_axis=0, ti...  41.8 us
    sub x2, matrix products, attend_one(): weights = jnp.where(allowed, jnp.exp(masked - peak), 0.0)  25 us
    dot_general x1, matrix products, add_products(): jnp.dot(columns, pieces[0], preferred_element_type=jnp.float32)  23.4 us
    dot_general x2, matrix products, attend_one(): jnp.einsum('kgst,tkd->skgd', probs, values, preferred_element_type=jnp.fl...  22.2 us
    another operation x2, other arithmetic  19.2 us
  transfers between devices with their start and end apart: 8, of which 4 were waited for; matrix products, arithmetic and copies ran while one was open for 7% of the time, Pallas kernels for 0%

profile of v1, /device:TPU:2, one launch (start us, length us, event | category | flops | bytes accessed | tf_op | source)
XLA Modules:
  0.0 690.0 jit_solution(498607041915075741)
XLA Ops:
  7.3 0.8 broadcast_compare_fusion.1
  8.1 1.3 gather_fusion.7
  9.3 1.3 gather_fusion.8
  10.6 0.9 convert_reduce_fusion
  11.6 0.8 select_reduce_fusion
  12.6 11.1 %gather_fusion.1 = bf16[20,64,3584]{2,1,0:T(8,128)(2,1)} fusion(bf16[32,64,3584]{2,1,0:T(8,128)(2,1)} %param.17, s32[1024]{0:T(1024)S(1)} %get-tuple-element.67), kind=kCustom, calls=%fused_computation.6 | custom fusion | bytes 18350160 | tf_op jit(solution)/shard_map/jit(_take)/gather | solution.py:32
  23.7 8.2 %select_select_fusion = bf16[20,64,3584]{2,1,0:T(8,128)(2,1)} fusion(bf16[20,64,3584]{2,1,0:T(8,128)(2,1)} %gather_fusion.1, pred[20]{0:T(512)(128)(4,1)S(1)} %compare_and_fusion.5, pred[20]{0:T(512)(128)(4,1)S(1)} %fusion.43), kind=kLoop, calls=%fused_computation.45 | loop fusion | flops 9175040 | bytes 18350120 | tf_op jit(solution)/shard_map/jit(_where)/select_n | solution.py:33
  32.0 5.9 all-to-all-start
  37.9 0.7 all-gather.6.cloned.1.call-update
  38.6 0.7 all-gather.4.cloned.1.call-update
  43.3 1.1 broadcast_select_fusion.2
  44.4 193.7 %all-to-all-done = bf16[20,64,3584]{2,1,0:T(8,128)(2,1)} async-done(((bf16[20,64,3584]{2,1,0:T(8,128)(2,1)}), bf16[20,64,3584]{2,1,0:T(8,128)(2,1)}, u32[]{:S(2)}, u32[]{:S(2)}) %all-to-all-start) | async-done | bytes 9175072 | tf_op jit(solution)/shard_map/all_to_all | solution.py:101
  238.1 4.3 all-to-all-start.2
  242.3 7.6 %gather_fusion.2 = bf16[16,64,3584]{2,1,0:T(8,128)(2,1)} fusion(bf16[20,64,3584]{2,1,0:T(8,128)(2,1)} %all-to-all-done, s32[1024]{0:T(1024)S(1)} %pad_clamp_fusion.2), kind=kCustom, calls=%fused_computation.7 | custom fusion | bytes 14680128 | tf_op jit(solution)/shard_map/jit(_take)/gather | solution.py:105
  250.0 3.8 broadcast_select_fusion
  253.8 1.0 fusion.41
  254.8 1.0 fusion.40
  255.8 1.0 fusion.39
  256.8 1.0 fusion.38
  257.8 1.1 fusion.37
  258.9 1.1 fusion.36
  259.9 1.0 fusion.35
  260.9 1.0 fusion.34
  261.9 5.3 all-to-all-start.1
  268.0 0.8 broadcast_compare_fusion
  268.8 2.1 multiply_cosine_fusion
  271.0 3.8 copy.60
  274.9 3.8 copy.59
  278.7 69.9 %all-to-all-done.1 = bf16[8,2,64,3584]{3,2,1,0:T(8,128)(2,1)} async-done(((bf16[8,2,64,3584]{3,2,1,0:T(8,128)(2,1)}), bf16[8,2,64,3584]{3,2,1,0:T(8,128)(2,1)}, u32[]{:S(2)}, u32[]{:S(2)}) %all-to-all-start.1) | async-done | bytes 7340064 | tf_op jit(solution)/shard_map/all_to_all | solution.py:109
  348.6 3.7 copy.57
  352.3 2.0 fusion.30
  354.4 0.8 copy-done.7
  355.2 2.4 fusion.49
  358.1 1.2 pad_maximum_fusion.2
  359.3 3.4 convolution_convert_fusion
  362.6 17.9 %copy.61 = bf16[1792,3584]{1,0:T(8,128)(2,1)} copy(bf16[1792,3584]{0,1:T(8,128)(2,1)} %bitcast.146) | data formatting | bytes 25690112 | tf_op jit(solution)/shard_map/dot_general | solution.py:38
  380.6 23.4 %fusion.47 = f32[2,576,14,128]{3,1,2,0:T(8,128)} fusion(bf16[14,128,3584,1]{2,1,0,3:T(8,128)(2,1)} %bitcast.147, f32[3584]{0:T(1024)S(1)} %convert_element_type.66, f32[2,576]{1,0:T(2,128)S(1)} %add_rsqrt_fusion, bf16[2,64,3584]{2,1,0:T(8,128)(2,1)S(1)} %bitcast.152, bf16[2,512,3584]{2,1,0:T(8,128)(2,1)} %bitcast.143), kind=kOutput, calls=%fused_computation.133 | convolution fusion | flops 14826405888 | bytes 29379072 | tf_op jit(solution)/shard_map/dot_general | solution.py:38
  403.9 18.8 %subtract_convert_fusion = (bf16[2,576,14,64]{3,1,2,0:T(8,128)(2,1)S(1)}, bf16[2,576,14,64]{3,1,2,0:T(8,128)(2,1)S(1)}) fusion(f32[2,576,14,128]{3,1,2,0:T(8,128)} %fusion.47, f32[2,576,64]{2,1,0:T(8,128)S(1)} %get-tuple-element.62, f32[2,576,64]{2,1,0:T(8,128)S(1)} %get-tuple-element.61), kind=kLoop, calls=%fused_computation.49 | loop fusion | flops 8257536 | bytes 12976128 | tf_op jit(solution)/shard_map/convert.2
  422.7 4.3 pad_maximum_fusion.1
  427.0 69.1 %while.10 = (s32[]{:T(128)}, bf16[2,576,1792]{2,1,0:T(8,128)(2,1)}, bf16[2,576,2,128]{3,1,2,0:T(8,128)(2,1)}, s32[2]{0:T(128)S(1)}, bf16[2,576,2,128]{3,1,2,0:T(...) while((s32[]{:T(128)}, bf16[2,576,1792]{2,1,0:T(8,128)(2,1)}, ...), condition=%wide.region_9.12_spmd, body=%wide.region_6.11_spmd.sunk | while | flops 2412382464 | bytes 61592804 | solution.py:153
  427.0 1.7 constant_dynamic-slice_fusion.2
  430.2 12.5 %fusion.74 = (f32[2,7,576]{2,1,0:T(8,128)S(1)}, f32[2,7,576,576]{2,3,1,0:T(8,128)}) fusion(pred[576,576]{0,1:T(8,128)(4,1)S(1)} %fusion.73, bf16[576,2,7,128]{3,0,2,1:T(8,128)(2,1)S(1)} %bitcast.139, bf16[2,576,2,128]{3,1,2,0:T(8,128)(2,1)S(1)} %get-tuple-element.128, s32[]{:T(128)} %get-tuple-element.117), kind=kOutput, calls=%fused_computation.135.clone.1 | convolution fusion | flops 1212310016 | bytes 21708292 | tf_op jit(solution)/shard_map/while/body/eval_jaxpr/sub | solution.py:56
  442.7 11.1 %convert_bitcast_fusion.2 = bf16[576,2,7,128]{3,0,2,1:T(8,128)(2,1)S(1)} fusion(f32[2,7,576,576]{2,3,1,0:T(8,128)} %get-tuple-element.108, f32[2,7,576]{2,1,0:T(8,128)S(1)} %get-tuple-element.109, bf16[2,576,2,128]{3,1,2,0:T(8,128)(2,1)} %get-tuple-element.126, s32[]{:T(128)} %get-tuple-element.117), kind=kOutput, calls=%fused_computation.19.clone.1 | convolution fusion | flops 1199407104 | bytes 23035904 | tf_op jit(solution)/shard_map/while/body/eval_jaxpr/kgst,tkd->skgd/dot_general | solution.py:58
  453.8 1.4 copy.75
  455.1 3.3 convert_element_type.102
  458.5 3.0 constant_dynamic-update-slice_fusion.2
  461.5 1.7 constant_dynamic-slice_fusion.2
  464.7 12.5 %fusion.74 = (f32[2,7,576]{2,1,0:T(8,128)S(1)}, f32[2,7,576,576]{2,3,1,0:T(8,128)}) fusion(pred[576,576]{0,1:T(8,128)(4,1)S(1)} %fusion.73, bf16[576,2,7,128]{3,0,2,1:T(8,128)(2,1)S(1)} %bitcast.139, bf16[2,576,2,128]{3,1,2,0:T(8,128)(2,1)S(1)} %get-tuple-element.128, s32[]{:T(128)} %get-tuple-element.117), kind=kOutput, calls=%fused_computation.135.clone.1 | convolution fusion | flops 1212310016 | bytes 21708292 | tf_op jit(solution)/shard_map/while/body/eval_jaxpr/sub | solution.py:56
  477.2 11.1 %convert_bitcast_fusion.2 = bf16[576,2,7,128]{3,0,2,1:T(8,128)(2,1)S(1)} fusion(f32[2,7,576,576]{2,3,1,0:T(8,128)} %get-tuple-element.108, f32[2,7,576]{2,1,0:T(8,128)S(1)} %get-tuple-element.109, bf16[2,576,2,128]{3,1,2,0:T(8,128)(2,1)} %get-tuple-element.126, s32[]{:T(128)} %get-tuple-element.117), kind=kOutput, calls=%fused_computation.19.clone.1 | convolution fusion | flops 1199407104 | bytes 23035904 | tf_op jit(solution)/shard_map/while/body/eval_jaxpr/kgst,tkd->skgd/dot_general | solution.py:58
  488.3 1.4 copy.75
  489.7 3.3 convert_element_type.102
  493.0 3.0 constant_dynamic-update-slice_fusion.2
  496.0 6.4 copy.62
  502.5 5.7 broadcast_select_fusion.1
  508.2 5.9 all-to-all-start.3
  514.4 41.8 %all-to-all-done.3 = bf16[2,512,1792]{2,0,1:T(2,128)(2,1)} async-done(((bf16[2,512,1792]{2,0,1:T(2,128)(2,1)}), bf16[2,512,1792]{2,0,1:T(2,128)(2,1)}, u32[]{:S(2)}, u32[]{:S(2)}) %all-to-all-start.3) | async-done | bytes 3670048 | tf_op jit(solution)/shard_map/all_to_all | solution.py:157
  556.3 2.5 copy.63
  558.7 2.1 copy.64
  560.8 5.3 gather_fusion.4
  566.1 5.1 select_select_fusion.1
  571.3 4.9 all-to-all-start.4
  576.2 0.8 slice.27
  577.7 100.6 %all-to-all-done.4 = bf16[20,64,1792]{2,1,0:T(8,128)(2,1)} async-done(((bf16[20,64,1792]{2,1,0:T(8,128)(2,1)}), bf16[20,64,1792]{2,1,0:T(8,128)(2,1)}, u32[]{:S(2)}, u32[]{:S(2)}) %all-to-all-start.4) | async-done | bytes 4587552 | tf_op jit(solution)/shard_map/all_to_all | solution.py:162
  678.3 4.9 copy.93
  (87 shorter events, 9.4 us)
Async XLA Ops:
  7.2 35.5 %copy-start = (bf16[32,8,3584]{2,1,0:T(8,128)(2,1)S(1)}, bf16[32,8,3584]{2,1,0:T(8,128)(2,1)}, u32[]{:S(2)}) copy-start(bf16[32,8,3584]{2,1,0:T(8,128)(2,1)} %param.19) | copy-start | bytes 5505028
  7.2 16.5 %copy-start.11 = (s32[20]{0:T(128)}, s32[20]{0:T(128)S(1)}, u32[]{:S(2)}) copy-start(s32[20]{0:T(128)S(1)} %and_select_fusion.1) | copy-start | bytes 244
  7.2 16.5 %copy-start.13 = (s32[20]{0:T(128)}, s32[20]{0:T(128)S(1)}, u32[]{:S(2)}) copy-start(s32[20]{0:T(128)S(1)} %and_select_fusion.3) | copy-start | bytes 244
  32.0 8.8 %copy-start.2 = (s32[64,1]{0,1:T(1,128)S(1)}, s32[64,1]{0,1:T(1,128)}, u32[]{:S(2)}) copy-start(s32[64,1]{0,1:T(1,128)} %param.20) | copy-start | bytes 772
  32.0 9.4 %copy-start.3 = (s32[64]{0:T(128)S(1)}, s32[64]{0:T(128)}, u32[]{:S(2)}) copy-start(s32[64]{0:T(128)} %param.22) | copy-start | bytes 772
  32.0 206.1 %all-to-all-start = ((bf16[20,64,3584]{2,1,0:T(8,128)(2,1)}), bf16[20,64,3584]{2,1,0:T(8,128)(2,1)}, u32[]{:S(2)}, u32[]{:S(2)}) async-start(bf16[20,64,3584]{2,1,0:T(8,128)(2,1)} %select_select_fusion), calls=%async_computation | async-start | bytes 18350080 | tf_op jit(solution)/shard_map/all_to_all | solution.py:101
  37.8 233.2 %all-gather.6.cloned.1.call-start = ((), (), s32[]{:S(2)}) async-start(), calls=%async_computation.6 | async-start | bytes 2064384 | tf_op jit(solution)/shard_map/all_gather | solution.py:137
  38.6 236.3 %all-gather.4.cloned.1.call-start = ((), (), s32[]{:S(2)}) async-start(), calls=%async_computation.5 | async-start | bytes 2064384 | tf_op jit(solution)/shard_map/all_gather | solution.py:138
  39.3 323.3 %all-gather.8.cloned.1.call-start = ((), (), s32[]{:S(2)}) async-start(), calls=%async_computation.7 | async-start | bytes 14450688 | tf_op jit(solution)/shard_map/all_gather | solution.py:136
  238.1 23.9 %all-to-all-start.2 = ((bf16[16,8,3584]{2,1,0:T(8,128)(2,1)}), bf16[16,8,3584]{2,1,0:T(8,128)(2,1)S(1)}, u32[]{:S(2)}, u32[]{:S(2)}) async-start(bf16[16,8,3584]{2,1,0:T(8,128)(2,1)} %broadcast_select_fusion.2), calls=%async_computation.2 | async-start | bytes 1835008 | tf_op jit(solution)/shard_map/all_to_all | solution.py:114
  261.9 5.3 copy-start.10
  261.9 5.4 copy-start.4
  261.9 86.7 %all-to-all-start.1 = ((bf16[8,2,64,3584]{3,2,1,0:T(8,128)(2,1)}), bf16[8,2,64,3584]{3,2,1,0:T(8,128)(2,1)}, u32[]{:S(2)}, u32[]{:S(2)}) async-start(bf16[8,2,64,3584]{3,2,1,0:T(8,128)(2,1)} %fusion.34), calls=%async_computation.1 | async-start | bytes 14680064 | tf_op jit(solution)/shard_map/all_to_all | solution.py:109
  352.3 6.9 %copy-start.5 = (bf16[8,2,64,3584]{3,2,0,1:T(8,128)(2,1)}, bf16[8,2,64,3584]{3,2,0,1:T(8,128)(2,1)S(1)}, u32[]{:S(2)}) copy-start(bf16[8,2,64,3584]{3,2,0,1:T(8,128)(2,1)S(1)} %copy.57) | copy-start | bytes 22020100
  352.3 2.9 copy-start.7
  355.2 4.1 copy-start.6
  422.7 4.3 copy-start.8
  496.0 6.5 copy-start.9
  502.5 11.7 %copy-start.12 = (s32[20]{0:T(128)S(1)}, s32[20]{0:T(128)}, u32[]{:S(2)}) copy-start(s32[20]{0:T(128)} %copy-done.11) | copy-start | bytes 244
  502.5 11.7 %copy-start.14 = (s32[20]{0:T(128)S(1)}, s32[20]{0:T(128)}, u32[]{:S(2)}) copy-start(s32[20]{0:T(128)} %copy-done.13) | copy-start | bytes 244
  502.5 11.7 %copy-start.15 = (s32[16]{0:T(128)S(1)}, s32[16]{0:T(128)}, u32[]{:S(2)}) copy-start(s32[16]{0:T(128)} %get-tuple-element.65) | copy-start | bytes 196
  502.5 11.7 %copy-start.16 = (s32[16]{0:T(128)S(1)}, s32[16]{0:T(128)}, u32[]{:S(2)}) copy-start(s32[16]{0:T(128)} %get-tuple-element.66) | copy-start | bytes 196
  508.2 48.0 %all-to-all-start.3 = ((bf16[2,512,1792]{2,0,1:T(2,128)(2,1)}), bf16[2,512,1792]{2,0,1:T(2,128)(2,1)}, u32[]{:S(2)}, u32[]{:S(2)}) async-start(bf16[2,512,1792]{2,0,1:T(2,128)(2,1)} %broadcast_select_fusion.1), calls=%async_computation.3 | async-start | bytes 7340032 | tf_op jit(solution)/shard_map/all_to_all | solution.py:157
  566.1 10.1 %copy-start.17 = (bf16[1792]{0:T(1024)(128)(2,1)S(1)}, bf16[1792]{0:T(1024)(128)(2,1)}, u32[]{:S(2)}) copy-start(bf16[1792]{0:T(1024)(128)(2,1)} %param.27) | copy-start | bytes 10756
  566.1 117.1 %copy-start.1 = (bf16[32,8,3584]{2,1,0:T(8,128)(2,1)S(1)}, bf16[32,8,3584]{2,1,0:T(8,128)(2,1)}, u32[]{:S(2)}) copy-start(bf16[32,8,3584]{2,1,0:T(8,128)(2,1)} %param.19) | copy-start | bytes 5505028
  571.3 107.1 %all-to-all-start.4 = ((bf16[20,64,1792]{2,1,0:T(8,128)(2,1)}), bf16[20,64,1792]{2,1,0:T(8,128)(2,1)}, u32[]{:S(2)}, u32[]{:S(2)}) async-start(bf16[20,64,1792]{2,1,0:T(8,128)(2,1)} %select_select_fusion.1), calls=%async_computation.4 | async-start | bytes 9175040 | tf_op jit(solution)/shard_map/all_to_all | solution.py:162
Sparse Core Ops, SparseCore 0:
  40.5 28.0 all-gather.5
  70.5 26.6 all-gather.3
  99.1 73.0 all-gather.7
